TPU v7x, 32 devices: a whole 2x2x4 slice. The times are simulated.
32 devices in a mesh: sx: 8 (over y, x, core), sy: 4 (over z).
Axes of the slice: x: 2, y: 2, z: 4, core: 2. Of those that a mesh axis runs over, the one named last changes fastest.
Arguments:
- coeffs: float32 [2, 8, 16, 4, 128, 128], P(None, 'sx', None, 'sy'), may hold values from -6 to 6
- deform: float32 [2, 4], replicated, may hold values from -0.08 to 0.08
Outputs:
- spectrum: float32 [2, 128, 512, 128], P(None, 'sx', 'sy')
All inputs are finite; a program needn't handle non-finite values.
Results may differ from a plain program's by a relative error of at most 0.0014.
Values sent between devices are 32-bit elements; how exact they have to be, the bound alone decides.
A program may use at most 64 MiB of HBM per device.

v0:
```python
import functools
import math

import jax
import jax.numpy as jnp
import numpy as np
from jax import lax
from jax.experimental import pallas as pl
from jax.experimental.pallas import tpu as pltpu
from jax.sharding import PartitionSpec as P

NODES = 4
RHS = 8
ROWS = 8
MESH = pl.DeviceIdType.MESH


def cheb_nodes(count):
    return (1.0 - np.cos(np.pi * (2.0 * np.arange(count) + 1.0) / (2.0 * count))) / 2.0


def lagrange_table(count):
    nodes = cheb_nodes(count)
    table = np.ones((count, 2, count))
    for row in range(count):
        for sibling in range(2):
            spots = (sibling + nodes) / 2.0
            for other in range(count):
                if other != row:
                    table[row, sibling] *= (spots - nodes[other]) / (nodes[row] - nodes[other])
    return table


def mix_matrix(along, right_sides, count):
    table = lagrange_table(count)
    blocks = []
    for sibling in range(2):
        weights = table[:, sibling].T
        eye = np.eye(count)
        inner = np.kron(weights, eye) if along == 0 else np.kron(eye, weights)
        blocks.append(np.kron(np.eye(right_sides), inner))
    return (np.concatenate(blocks, axis=0) * math.sqrt(0.5)).astype(np.float32)


TAYLOR_SIN = [((-1.0) ** k) * (2.0 * math.pi) ** (2 * k + 1) / math.factorial(2 * k + 1) for k in range(8)]
TAYLOR_COS = [((-1.0) ** k) * (2.0 * math.pi) ** (2 * k) / math.factorial(2 * k) for k in range(8)]


def horner(coefs, u):
    acc = coefs[-1] * u + coefs[-2]
    for c in coefs[-3::-1]:
        acc = acc * u + c
    return acc


def turns(t):
    half = jnp.floor(2.0 * t + 0.5)
    rest = t - 0.5 * half
    parity = half - 2.0 * jnp.floor(0.5 * half)
    sign = 1.0 - 2.0 * parity
    u = rest * rest
    return sign * horner(TAYLOR_COS, u), sign * rest * horner(TAYLOR_SIN, u)


def split_index(value, by):
    return lax.div(value, by), lax.rem(value, by)


def plan_of(space_x, space_y):
    steps = []
    sx, sy, row = space_x, space_y, 0
    while sx > 1 or sy > 1:
        if sx > 1:
            steps.append((0, sx, sy, row))
            row += max(8, sx * sy)
            sx //= 2
        if sy > 1:
            steps.append((1, sx, sy, row))
            row += max(8, sx * sy)
            sy //= 2
    return steps, row


def kernel(
    dims,
    deform_hbm,
    mix_hbm,
    coeffs_ref,
    out_ref,
    recv,
    twid,
    base1,
    base2,
    last1,
    last2,
    lhs_high,
    lhs_low,
    state,
    send_sem,
    recv_sem,
    deform_ref,
    mix_ref,
    deform_sem,
    mix_sem,
    plane_sem,
):
    space_x, space_y, local_x, local_y, rows, modes = dims
    steps, _ = plan_of(space_x, space_y)
    chunks_y = local_y // rows
    chunks = local_x * chunks_y
    boxes = space_x * space_y
    gain_x, gain_y = space_x, space_y
    mx = lax.axis_index("sx")
    my = lax.axis_index("sy")
    me = mx * space_y + my

    barrier = pltpu.get_barrier_semaphore()

    for o in range(1, space_y):
        pl.semaphore_signal(
            barrier, inc=1, device_id=(mx, lax.rem(my + o, space_y)), device_id_type=MESH
        )
    for o in range(1, space_x):
        pl.semaphore_signal(
            barrier, inc=1, device_id=(lax.rem(mx + o, space_x), my), device_id_type=MESH
        )
    fetch_mix = pltpu.make_async_copy(mix_hbm, mix_ref, mix_sem)
    fetch_mix.start()
    fetch_deform = pltpu.make_async_copy(deform_hbm, deform_ref, deform_sem)
    fetch_deform.start()
    fetch_deform.wait()

    lane = lax.broadcasted_iota(jnp.int32, (1, 128), 1)
    spots = [float(q) for q in cheb_nodes(NODES)]

    def node_of(index):
        node = jnp.full((1, 128), spots[0], jnp.float32)
        for t in range(1, NODES):
            node = jnp.where(index == t, spots[t], node)
        return node

    node_x = node_of(lane // NODES % NODES)
    node_y = node_of(lane % NODES)

    def warped(sx, sy, count):
        box = lax.broadcasted_iota(jnp.int32, (count, 128), 0)
        ax = (box // sy).astype(jnp.float32)
        ay = (box % sy).astype(jnp.float32)
        p1 = (ax + node_x) / sx
        p2 = (ay + node_y) / sy
        y1, y2 = 0.0, 0.0
        for m in range(modes):
            y1 = y1 + deform_ref[0, m] * turns((p1 + p2) * (0.5 * (m + 1)))[1]
            y2 = y2 + deform_ref[1, m] * turns((p1 - p2) * (0.5 * (m + 1)))[1]
        return p1 + y1, p2 + y2

    for along, sx, sy, row in steps[1:]:
        count = max(8, sx * sy)
        y1, y2 = warped(sx, sy, count)
        c, s = turns((y1 * (0.25 * sx)) if along == 0 else (y2 * (0.25 * sy)))
        twid[0, pl.ds(row, count), :] = c
        twid[1, pl.ds(row, count), :] = s

    y1, y2 = warped(space_x, space_y, boxes)
    for fx in range(local_x):
        for child in range(2):
            freq = (mx * local_x + fx).astype(jnp.float32) + (0.25 + 0.5 * child)
            c, s = turns(y1 * (freq * gain_x))
            base1[0, 2 * fx + child] = c
            base1[1, 2 * fx + child] = s
    twid[0, pl.ds(0, boxes), :] = y2

    def base_box(i, _):
        freq = lax.broadcasted_iota(jnp.int32, (local_y, 128), 0) + my * local_y
        warp = twid[0, pl.ds(i, 1), :]
        c, s = turns(warp * ((freq.astype(jnp.float32) + 0.5) * gain_y))
        base2[0, i] = c
        base2[1, i] = s
        return 0

    lax.fori_loop(0, boxes, base_box, 0)

    y1, y2 = warped(1, 1, 8)
    out_x = local_x * space_x
    freq = lax.broadcasted_iota(jnp.int32, (out_x, 128), 0) + mx * out_x
    c, s = turns(y1[0:1] * (freq.astype(jnp.float32) + 0.5))
    last1[0] = c
    last1[1] = s
    for child in range(space_y):
        freq = (lax.broadcasted_iota(jnp.int32, (local_y, 128), 0) + my * local_y) * space_y + child
        c, s = turns(y2[0:1] * (freq.astype(jnp.float32) + 0.5))
        last2[0, child] = c
        last2[1, child] = s

    def piece(k, px, py):
        fx, fy = split_index(k, chunks_y)
        start = pl.multiple_of(py * local_y + fy * rows, 8)
        return coeffs_ref.at[:, 0, px * local_x + fx, 0, pl.ds(start, rows), :]

    def send(k, px, py):
        pltpu.make_async_remote_copy(
            src_ref=piece(k, px, py),
            dst_ref=recv.at[k, me],
            send_sem=send_sem.at[k],
            recv_sem=recv_sem.at[k],
            device_id=(px, py),
            device_id_type=MESH,
        ).start()

    pl.semaphore_wait(barrier, space_x + space_y - 2)
    for o in range(1, space_x):
        pl.semaphore_signal(
            plane_sem, inc=1, device_id=(lax.rem(mx + o, space_x), my), device_id_type=MESH
        )

    def send_line(k, _):
        for o in range(1, space_y):
            send(k, mx, lax.rem(my + o, space_y))
        return 0

    lax.fori_loop(0, chunks, send_line, 0)
    pl.semaphore_wait(plane_sem, space_x - 1)

    def send_chunk(k, _):
        def send_one(i, _):
            oy, ox = split_index(i, space_x - 1)
            send(k, lax.rem(mx + 1 + ox, space_x), lax.rem(my + 1 + oy, space_y))
            return 0

        lax.fori_loop(0, boxes - space_y, send_one, 0)
        pltpu.make_async_copy(piece(k, mx, my), recv.at[k, me], recv_sem.at[k]).start()
        return 0

    lax.fori_loop(0, chunks, send_chunk, 0)
    fetch_mix.wait()

    def rotate_into(slot, pair, sibling, size, re0, im0, re1, im1):
        spot = (slot, pl.ds(pair * 4 * size, 4 * size), pl.ds(128 * sibling, 128))
        whole = jnp.concatenate([re0, im0, re1, im1], axis=0)
        high = whole.astype(jnp.bfloat16)
        lhs_high[spot] = high
        lhs_low[spot] = (whole - high.astype(jnp.float32)).astype(jnp.bfloat16)

    def pair_of(along, sy, a1, a2):
        if along == 0:
            return (a1 // 2) * sy + a2, a1 % 2
        return a1 * (sy // 2) + a2 // 2, a2 % 2

    def compute(k, _):
        pltpu.make_async_copy(recv.at[k], recv.at[k], recv_sem.at[k]).wait()
        fx, fy = split_index(k, chunks_y)
        fy_rows = pl.ds(pl.multiple_of(fy * rows, 8), rows)
        size = rows
        for number, (along, sx, sy, row) in enumerate(steps):
            slot = number % 2
            for a1 in range(sx):
                for a2 in range(sy):
                    box = a1 * sy + a2
                    pair, sibling = pair_of(along, sy, a1, a2)
                    if number == 0:
                        re, im = recv[k, box, 0], recv[k, box, 1]
                        c, s = base2[0, box, fy_rows, :], base2[1, box, fy_rows, :]
                        re, im = re * c + im * s, im * c - re * s
                        c, s = base1[0, 2 * fx, pl.ds(box, 1), :], base1[1, 2 * fx, pl.ds(box, 1), :]
                        re0, im0 = re * c + im * s, im * c - re * s
                        c, s = base1[0, 2 * fx + 1, pl.ds(box, 1), :], base1[1, 2 * fx + 1, pl.ds(box, 1), :]
                        re1, im1 = re * c + im * s, im * c - re * s
                    else:
                        at = box * 2 * size
                        half = size // 2
                        re = jnp.concatenate(
                            [state[pl.ds(at, half), :], state[pl.ds(at + 2 * half, half), :]], axis=0
                        )
                        im = jnp.concatenate(
                            [state[pl.ds(at + half, half), :], state[pl.ds(at + 3 * half, half), :]], axis=0
                        )
                        c, s = twid[0, pl.ds(row + box, 1), :], twid[1, pl.ds(row + box, 1), :]
                        rc, rs, ic, js = re * c, re * s, im * c, im * s
                        re0, im0 = rc - js, ic + rs
                        re1, im1 = rc + js, ic - rs
                    rotate_into(slot, pair, sibling, size, re0, im0, re1, im1)
            by_high = jnp.dot(lhs_high[slot], mix_ref[along], preferred_element_type=jnp.float32)
            by_low = jnp.dot(lhs_low[slot], mix_ref[along, :, 0:128], preferred_element_type=jnp.float32)
            state[...] = by_high[:, 0:128] + (by_high[:, 128:256] + by_low)
            size *= 2
        total = len(steps)
        for code in range(1 << total):
            bits = [(code >> n) & 1 for n in range(total)]
            at = 0
            for n in range(total - 1):
                at += bits[n] * rows * (1 << n)
            half = rows * (1 << (total - 1))
            at += bits[total - 1] * 2 * half
            bx, by = 0, 0
            for n, (along, _, _, _) in enumerate(steps):
                if along == 0:
                    bx = 2 * bx + bits[n]
                else:
                    by = 2 * by + bits[n]
            re = state[pl.ds(at, rows), :]
            im = state[pl.ds(at + half, rows), :]
            first = fx * space_x + bx
            c1, s1 = last1[0, pl.ds(first, 1), :], last1[1, pl.ds(first, 1), :]
            c2, s2 = last2[0, by, fy_rows, :], last2[1, by, fy_rows, :]
            c = c1 * c2 - s1 * s2
            s = s1 * c2 + c1 * s2
            spots = pl.ds(fy * (rows * space_y) + by, rows, stride=space_y)
            out_ref[0, first, spots, :] = re * c - im * s
            out_ref[1, first, spots, :] = im * c + re * s
        return 0

    lax.fori_loop(0, chunks, compute, 0)

    def drain(k, _):
        sent = recv.at[k, pl.ds(0, boxes - 1)]
        pltpu.make_async_copy(sent, sent, send_sem.at[k]).wait()
        return 0

    lax.fori_loop(0, chunks, drain, 0)


def body(coeffs, deform):
    space_x, space_y = lax.axis_size("sx"), lax.axis_size("sy")
    _, _, freq_x, _, freq_y, lanes = coeffs.shape
    local_x, local_y = freq_x // space_x, freq_y // space_y
    rows = ROWS
    chunks = local_x * local_y // rows
    boxes = space_x * space_y
    out_x, out_y = local_x * space_x, local_y * space_y
    right_sides = lanes // NODES**2
    mix = np.stack([mix_matrix(0, right_sides, NODES), mix_matrix(1, right_sides, NODES)])
    high = mix.astype(jnp.bfloat16)
    low = (mix - high.astype(np.float32)).astype(jnp.bfloat16)
    mix = jnp.asarray(np.concatenate([high, low], axis=2))
    _, twid_rows = plan_of(space_x, space_y)
    dims = (space_x, space_y, local_x, local_y, rows, deform.shape[1])
    vmem = pl.BlockSpec(memory_space=pltpu.VMEM)
    state_rows = boxes * 2 * rows
    f32 = jnp.float32
    return pl.pallas_call(
        functools.partial(kernel, dims),
        out_shape=pltpu.VMEM((2, out_x, out_y, lanes), f32),
        in_specs=[
            pl.BlockSpec(memory_space=pl.ANY),
            pl.BlockSpec(memory_space=pl.ANY),
            pl.BlockSpec(memory_space=pl.ANY),
        ],
        out_specs=vmem,
        scratch_shapes=[
            pltpu.VMEM((chunks, boxes, 2, rows, lanes), f32),
            pltpu.VMEM((2, twid_rows, lanes), f32),
            pltpu.VMEM((2, 2 * local_x, boxes, lanes), f32),
            pltpu.VMEM((2, boxes, local_y, lanes), f32),
            pltpu.VMEM((2, out_x, lanes), f32),
            pltpu.VMEM((2, space_y, local_y, lanes), f32),
            pltpu.VMEM((2, state_rows, 2 * lanes), jnp.bfloat16),
            pltpu.VMEM((2, state_rows, 2 * lanes), jnp.bfloat16),
            pltpu.VMEM((state_rows, lanes), f32),
            pltpu.SemaphoreType.DMA((chunks,)),
            pltpu.SemaphoreType.DMA((chunks,)),
            pltpu.SMEM(deform.shape, f32),
            pltpu.VMEM(mix.shape, mix.dtype),
            pltpu.SemaphoreType.DMA,
            pltpu.SemaphoreType.DMA,
            pltpu.SemaphoreType.REGULAR,
        ],
        compiler_params=pltpu.CompilerParams(collective_id=0, has_side_effects=True),
        name="butterfly",
    )(deform, mix, coeffs)


def solution(mesh):
    placed = (P(None, "sx", None, "sy", None, None), P())
    return jax.shard_map(
        body, mesh=mesh, in_specs=placed, out_specs=P(None, "sx", "sy", None), check_vma=False
    )
```

profile of v0, /device:TPU:0, one launch (start us, length us, event | category | flops | bytes accessed | tf_op | source)
XLA Modules:
  0.0 55.8 jit_solution(8084181189911083427)
XLA Ops:
  0.0 54.5 %butterfly.1 = f32[2,16,128,128]{3,2,1,0:T(8,128)S(1)} custom-call(f32[2,4]{1,0:T(2,128)} %deform_hbm.1, bf16[2,256,256]{2,1,0:T(8,128)(2,1)} %constant.2.clone.mix_hbm, f32[2,1,16,1,128,128]{5,4,3,2,1,0:T(8,128)} %coeffs_ref.1), custom_call_target="tpu_custom_call" | custom-call | tf_op jit(solution)/shard_map/butterfly/pallas_call | solution.py:340
  54.5 1.3 %copy.5 = f32[2,16,128,128]{3,2,1,0:T(8,128)} copy(f32[2,16,128,128]{3,2,1,0:T(8,128)S(1)} %butterfly.1) | data formatting | bytes 4194304
where the time goes:
time: 56 us; the launch traced here: 55.8 us
  Pallas kernels  54.5 us (97%)
  local copies, waits for them, and re-layouts  1.32 us (2%)
    pallas_call x1, Pallas kernels, body(): pl.pallas_call(functools.partial(kernel, dims), out_shape=pltpu.VMEM((2,...  54.5 us
    unnamed x1, local copies, waits for them, and re-layouts  1.32 us

commit v1 on v0

--- a/solution.py
+++ b/solution.py
@@ -103,6 +103,7 @@
     deform_sem,
     mix_sem,
     plane_sem,
+    go_sem,
 ):
     space_x, space_y, local_x, local_y, rows, modes = dims
     steps, _ = plan_of(space_x, space_y)
@@ -116,18 +117,92 @@
 
     barrier = pltpu.get_barrier_semaphore()
 
-    for o in range(1, space_y):
-        pl.semaphore_signal(
-            barrier, inc=1, device_id=(mx, lax.rem(my + o, space_y)), device_id_type=MESH
-        )
-    for o in range(1, space_x):
-        pl.semaphore_signal(
-            barrier, inc=1, device_id=(lax.rem(mx + o, space_x), my), device_id_type=MESH
-        )
+    half = space_y // 2
+    side, inner = split_index(my, half)
+    near_y = side * half
+    far_y = (1 - side) * half
+    low = side == 0
+
+    def signal(sem, px, py):
+        pl.semaphore_signal(sem, inc=1, device_id=(px, py), device_id_type=MESH)
+
+    for o in range(half):
+        signal(barrier, mx, far_y + lax.rem(inner + o, half))
+
+    @pl.when(low)
+    def _():
+        for o in range(1, half):
+            signal(barrier, mx, lax.rem(inner + o, half))
+        for o in range(1, space_x):
+            signal(barrier, lax.rem(mx + o, space_x), my)
+
     fetch_mix = pltpu.make_async_copy(mix_hbm, mix_ref, mix_sem)
     fetch_mix.start()
     fetch_deform = pltpu.make_async_copy(deform_hbm, deform_ref, deform_sem)
     fetch_deform.start()
+
+    def piece(k, px, py):
+        fx, fy = split_index(k, chunks_y)
+        start = pl.multiple_of(py * local_y + fy * rows, 8)
+        return coeffs_ref.at[:, 0, px * local_x + fx, 0, pl.ds(start, rows), :]
+
+    def send(k, px, py):
+        pltpu.make_async_remote_copy(
+            src_ref=piece(k, px, py),
+            dst_ref=recv.at[k, me],
+            send_sem=send_sem.at[k],
+            recv_sem=recv_sem.at[k],
+            device_id=(px, py),
+            device_id_type=MESH,
+        ).start()
+
+    @pl.when(low)
+    def _():
+        pl.semaphore_wait(barrier, space_y - 1 + space_x - 1)
+        for o in range(1, space_x):
+            signal(plane_sem, lax.rem(mx + o, space_x), my)
+
+    @pl.when(jnp.logical_not(low))
+    def _():
+        pl.semaphore_wait(barrier, half)
+
+    def send_line(k, _):
+        for o in range(half):
+            send(k, mx, far_y + lax.rem(inner + o, half))
+        return 0
+
+    lax.fori_loop(0, chunks, send_line, 0)
+
+    @pl.when(low)
+    def _():
+        pl.semaphore_wait(plane_sem, space_x - 1)
+
+    @pl.when(my == half - 1)
+    def _():
+        for o in range(half):
+            signal(go_sem, mx, half + o)
+
+    @pl.when(jnp.logical_not(low))
+    def _():
+        pl.semaphore_wait(go_sem, 1)
+
+    def send_chunk(k, _):
+        def send_far(i, _):
+            oy, ox = split_index(i, space_x - 1)
+            send(k, lax.rem(mx + 1 + ox, space_x), far_y + lax.rem(inner + oy, half))
+            return 0
+
+        def send_near(i, _):
+            oy, ox = split_index(i, space_x)
+            send(k, lax.rem(mx + 1 + ox, space_x), near_y + lax.rem(inner + 1 + oy, half))
+            return 0
+
+        lax.fori_loop(0, half * (space_x - 1), send_far, 0)
+        lax.fori_loop(0, half * space_x - 1, send_near, 0)
+        pltpu.make_async_copy(piece(k, mx, my), recv.at[k, me], recv_sem.at[k]).start()
+        return 0
+
+    lax.fori_loop(0, chunks, send_chunk, 0)
     fetch_deform.wait()
 
     lane = lax.broadcasted_iota(jnp.int32, (1, 128), 1)
@@ -192,46 +267,6 @@
         last2[0, child] = c
         last2[1, child] = s
 
-    def piece(k, px, py):
-        fx, fy = split_index(k, chunks_y)
-        start = pl.multiple_of(py * local_y + fy * rows, 8)
-        return coeffs_ref.at[:, 0, px * local_x + fx, 0, pl.ds(start, rows), :]
-
-    def send(k, px, py):
-        pltpu.make_async_remote_copy(
-            src_ref=piece(k, px, py),
-            dst_ref=recv.at[k, me],
-            send_sem=send_sem.at[k],
-            recv_sem=recv_sem.at[k],
-            device_id=(px, py),
-            device_id_type=MESH,
-        ).start()
-
-    pl.semaphore_wait(barrier, space_x + space_y - 2)
-    for o in range(1, space_x):
-        pl.semaphore_signal(
-            plane_sem, inc=1, device_id=(lax.rem(mx + o, space_x), my), device_id_type=MESH
-        )
-
-    def send_line(k, _):
-        for o in range(1, space_y):
-            send(k, mx, lax.rem(my + o, space_y))
-        return 0
-
-    lax.fori_loop(0, chunks, send_line, 0)
-    pl.semaphore_wait(plane_sem, space_x - 1)
-
-    def send_chunk(k, _):
-        def send_one(i, _):
-            oy, ox = split_index(i, space_x - 1)
-            send(k, lax.rem(mx + 1 + ox, space_x), lax.rem(my + 1 + oy, space_y))
-            return 0
-
-        lax.fori_loop(0, boxes - space_y, send_one, 0)
-        pltpu.make_async_copy(piece(k, mx, my), recv.at[k, me], recv_sem.at[k]).start()
-        return 0
-
-    lax.fori_loop(0, chunks, send_chunk, 0)
     fetch_mix.wait()
 
     def rotate_into(slot, pair, sibling, size, re0, im0, re1, im1):
@@ -363,6 +398,7 @@
             pltpu.SemaphoreType.DMA,
             pltpu.SemaphoreType.DMA,
             pltpu.SemaphoreType.REGULAR,
+            pltpu.SemaphoreType.REGULAR,
         ],
         compiler_params=pltpu.CompilerParams(collective_id=0, has_side_effects=True),
         name="butterfly",

time: 56 us -> 53.8 us (0.961)
  Pallas kernels: 54.5 us -> 52.3 us
    pallas_call x1, Pallas kernels: 54.5 us -> 52.3 us  [body(): pl.pallas_call(functools.partial(kernel, dims), out_shape=pltpu.VMEM((2,...]
where the time goes in v1:
time: 53.8 us; the launch traced here: 53.6 us
  Pallas kernels  52.3 us (97%)
  local copies, waits for them, and re-layouts  1.32 us (2%)
    pallas_call x1, Pallas kernels, body(): pl.pallas_call(functools.partial(kernel, dims), out_shape=pltpu.VMEM((2,...  52.3 us
    unnamed x1, local copies, waits for them, and re-layouts  1.32 us

profile of v1, /device:TPU:0, one launch (start us, length us, event | category | flops | bytes accessed | tf_op | source)
XLA Modules:
  0.0 53.6 jit_solution(1850857162770322755)
XLA Ops:
  0.0 52.3 %butterfly.1 = f32[2,16,128,128]{3,2,1,0:T(8,128)S(1)} custom-call(f32[2,4]{1,0:T(2,128)} %deform_hbm.1, bf16[2,256,256]{2,1,0:T(8,128)(2,1)} %constant.2.clone.mix_hbm, f32[2,1,16,1,128,128]{5,4,3,2,1,0:T(8,128)} %coeffs_ref.1), custom_call_target="tpu_custom_call" | custom-call | tf_op jit(solution)/shard_map/butterfly/pallas_call | solution.py:375
  52.3 1.3 %copy.5 = f32[2,16,128,128]{3,2,1,0:T(8,128)} copy(f32[2,16,128,128]{3,2,1,0:T(8,128)S(1)} %butterfly.1) | data formatting | bytes 4194304

commit v2 on v1

v2 whole, which is shorter than its diff:
```python
import functools
import math

import jax
import jax.numpy as jnp
import numpy as np
from jax import lax
from jax.experimental import pallas as pl
from jax.experimental.pallas import tpu as pltpu
from jax.sharding import PartitionSpec as P

NODES = 4
FIRST = 2
VMEM_ROOM = 67043328
RHS = 8
ROWS = 8
MESH = pl.DeviceIdType.MESH


def cheb_nodes(count):
    return (1.0 - np.cos(np.pi * (2.0 * np.arange(count) + 1.0) / (2.0 * count))) / 2.0


def lagrange_table(count):
    nodes = cheb_nodes(count)
    table = np.ones((count, 2, count))
    for row in range(count):
        for sibling in range(2):
            spots = (sibling + nodes) / 2.0
            for other in range(count):
                if other != row:
                    table[row, sibling] *= (spots - nodes[other]) / (nodes[row] - nodes[other])
    return table


def mix_matrix(along, right_sides, count):
    table = lagrange_table(count)
    blocks = []
    for sibling in range(2):
        weights = table[:, sibling].T
        eye = np.eye(count)
        inner = np.kron(weights, eye) if along == 0 else np.kron(eye, weights)
        blocks.append(np.kron(np.eye(right_sides), inner))
    return (np.concatenate(blocks, axis=0) * math.sqrt(0.5)).astype(np.float32)


TAYLOR_SIN = [((-1.0) ** k) * (2.0 * math.pi) ** (2 * k + 1) / math.factorial(2 * k + 1) for k in range(8)]
TAYLOR_COS = [((-1.0) ** k) * (2.0 * math.pi) ** (2 * k) / math.factorial(2 * k) for k in range(8)]


def horner(coefs, u):
    acc = coefs[-1] * u + coefs[-2]
    for c in coefs[-3::-1]:
        acc = acc * u + c
    return acc


def turns(t):
    half = jnp.floor(2.0 * t + 0.5)
    rest = t - 0.5 * half
    parity = half - 2.0 * jnp.floor(0.5 * half)
    sign = 1.0 - 2.0 * parity
    u = rest * rest
    return sign * horner(TAYLOR_COS, u), sign * rest * horner(TAYLOR_SIN, u)


def split_index(value, by):
    return lax.div(value, by), lax.rem(value, by)


def plan_of(space_x, space_y):
    steps = []
    sx, sy, row = space_x, space_y, 0
    while sx > 1 or sy > 1:
        if sx > 1:
            steps.append((0, sx, sy, row))
            row += max(8, sx * sy)
            sx //= 2
        if sy > 1:
            steps.append((1, sx, sy, row))
            row += max(8, sx * sy)
            sy //= 2
    return steps, row


def butterfly_steps(dims, refs):
    space_x, space_y, local_x, local_y, rows, _ = dims
    recv, twid, base1, base2, last1, last2, mix_ref, lhs_high, lhs_low, state = refs
    steps, _ = plan_of(space_x, space_y)
    split = max(n for n, step in enumerate(steps) if step[0] == 1)
    chunks_y = local_y // rows
    state_rows = space_x * space_y * 2 * rows

    def place(k):
        fx, fy = split_index(k, chunks_y)
        return fx, fy, pl.ds(pl.multiple_of(fy * rows, 8), rows)

    def rotate_into(slot, pair, sibling, size, re0, im0, re1, im1):
        spot = (slot, pl.ds(pair * 4 * size, 4 * size), pl.ds(128 * sibling, 128))
        whole = jnp.concatenate([re0, im0, re1, im1], axis=0)
        high = whole.astype(jnp.bfloat16)
        lhs_high[spot] = high
        lhs_low[spot] = (whole - high.astype(jnp.float32)).astype(jnp.bfloat16)

    def rotate(number, k, first_y, count_y):
        along, sx, sy, row = steps[number]
        fx, _, fy_rows = place(k)
        size = rows << number
        for a1 in range(sx):
            for j in range(count_y):
                table = a1 * sy + first_y + j
                if along == 0:
                    pair, sibling = (a1 // 2) * count_y + j, a1 % 2
                else:
                    pair, sibling = a1 * (count_y + 1 >> 1) + j // 2, j % 2
                if number == 0:
                    re, im = recv[k, table, 0], recv[k, table, 1]
                    c, s = base2[0, table, fy_rows, :], base2[1, table, fy_rows, :]
                    re, im = re * c + im * s, im * c - re * s
                    spot = pl.ds(table, 1)
                    c, s = base1[0, 2 * fx, spot, :], base1[1, 2 * fx, spot, :]
                    re0, im0 = re * c + im * s, im * c - re * s
                    c, s = base1[0, 2 * fx + 1, spot, :], base1[1, 2 * fx + 1, spot, :]
                    re1, im1 = re * c + im * s, im * c - re * s
                else:
                    at = (a1 * count_y + j) * 2 * size
                    half = size // 2
                    re = jnp.concatenate(
                        [state[pl.ds(at, half), :], state[pl.ds(at + 2 * half, half), :]], axis=0
                    )
                    im = jnp.concatenate(
                        [state[pl.ds(at + half, half), :], state[pl.ds(at + 3 * half, half), :]], axis=0
                    )
                    spot = pl.ds(row + table, 1)
                    c, s = twid[0, spot, :], twid[1, spot, :]
                    rc, rs, ic, js = re * c, re * s, im * c, im * s
                    re0, im0 = rc - js, ic + rs
                    re1, im1 = rc + js, ic - rs
                rotate_into(number % 2, pair, sibling, size, re0, im0, re1, im1)

    def mixed(number, count):
        slot, along = number % 2, steps[number][0]
        by_high = jnp.dot(
            lhs_high[slot, 0:count], mix_ref[along], preferred_element_type=jnp.float32
        )
        by_low = jnp.dot(
            lhs_low[slot, 0:count], mix_ref[along, :, 0:128], preferred_element_type=jnp.float32
        )
        return by_high[:, 0:128] + (by_high[:, 128:256] + by_low)

    def mixed_half(number, side):
        slot, along = number % 2, steps[number][0]
        deep = pl.ds(pl.multiple_of(side * 128, 128), 128)
        by_high = jnp.dot(
            lhs_high[slot, :, 0:128], mix_ref[along, deep, :], preferred_element_type=jnp.float32
        )
        by_low = jnp.dot(
            lhs_low[slot, :, 0:128], mix_ref[along, deep, 0:128], preferred_element_type=jnp.float32
        )
        return by_high[:, 0:128] + (by_high[:, 128:256] + by_low)

    def whole_step(number, k):
        rotate(number, k, 0, steps[number][2])
        state[...] = mixed(number, state_rows)

    def half_steps(k, side):
        for number in range(split):
            count_y = steps[number][2] // 2
            rotate(number, k, side * count_y, count_y)
            state[0 : state_rows // 2] = mixed(number, state_rows // 2)
        rotate(split, k, side, 1)
        return mixed_half(split, side)

    def finish(k, store):
        fx, fy, fy_rows = place(k)
        total = len(steps)
        ends = []
        for code in range(1 << total):
            bits = [(code >> n) & 1 for n in range(total)]
            at = 0
            for n in range(total - 1):
                at += bits[n] * rows * (1 << n)
            half = rows * (1 << (total - 1))
            at += bits[total - 1] * 2 * half
            bx, by = 0, 0
            for n, (along, _, _, _) in enumerate(steps):
                if along == 0:
                    bx = 2 * bx + bits[n]
                else:
                    by = 2 * by + bits[n]
            ends.append((bx, by, at, at + half))
        for bx, by, at_re, at_im in sorted(ends):
            re = state[pl.ds(at_re, rows), :]
            im = state[pl.ds(at_im, rows), :]
            first = fx * space_x + bx
            c1, s1 = last1[0, pl.ds(first, 1), :], last1[1, pl.ds(first, 1), :]
            c2, s2 = last2[0, by, fy_rows, :], last2[1, by, fy_rows, :]
            c = c1 * c2 - s1 * s2
            s = s1 * c2 + c1 * s2
            store(fx, fy, bx, by, re * c - im * s, im * c + re * s)

    return len(steps), split, whole_step, half_steps, finish


def kernel(
    dims,
    deform_hbm,
    mix_hbm,
    coeffs_ref,
    out_ref,
    recv,
    twid,
    base1,
    base2,
    last1,
    last2,
    mix_ref,
    near_ref,
    lhs_high,
    lhs_low,
    state,
    send_sem,
    recv_sem,
    deform_ref,
    deform_sem,
    mix_sem,
    plane_sem,
    go_sem,
    line_sem,
):
    space_x, space_y, local_x, local_y, rows, modes = dims
    steps, _ = plan_of(space_x, space_y)
    chunks_y = local_y // rows
    chunks = local_x * chunks_y
    boxes = space_x * space_y
    gain_x, gain_y = space_x, space_y
    mx = lax.axis_index("sx")
    my = lax.axis_index("sy")
    me = mx * space_y + my

    barrier = pltpu.get_barrier_semaphore()

    half = space_y // 2
    side, inner = split_index(my, half)
    near_y = side * half
    far_y = (1 - side) * half
    mirror = space_y - 1 - my
    hub = my == 0
    low = jnp.logical_and(side == 0, my > 0)
    high = side == 1

    def signal(sem, px, py):
        pl.semaphore_signal(sem, inc=1, device_id=(px, py), device_id_type=MESH)

    @pl.when(side == 0)
    def _():
        for o in range(half):
            signal(barrier, mx, half + lax.rem(inner + o, half))

    @pl.when(low)
    def _():
        signal(barrier, mx, 0)

    @pl.when(high)
    def _():
        signal(barrier, mx, mirror)

        @pl.when(mirror > 0)
        def _():
            signal(barrier, mx, 0)

    @pl.when(hub)
    def _():
        for o in range(1, space_x):
            signal(barrier, lax.rem(mx + o, space_x), 0)

    fetch_mix = pltpu.make_async_copy(mix_hbm, mix_ref, mix_sem)
    fetch_mix.start()
    fetch_deform = pltpu.make_async_copy(deform_hbm, deform_ref, deform_sem)
    fetch_deform.start()

    def piece(k, px, py):
        fx, fy = split_index(k, chunks_y)
        start = pl.multiple_of(py * local_y + fy * rows, 8)
        return coeffs_ref.at[:, 0, px * local_x + fx, 0, pl.ds(start, rows), :]

    def send(k, px, py, lane_sem=None):
        pltpu.make_async_remote_copy(
            src_ref=piece(k, px, py),
            dst_ref=recv.at[k, me],
            send_sem=send_sem.at[k],
            recv_sem=recv_sem.at[k if lane_sem is None else lane_sem],
            device_id=(px, py),
            device_id_type=MESH,
        ).start()

    def send_across(k, px, py):
        send(k, px, py, jnp.where(k == chunks - 1, chunks, k))

    def send_line(py):
        def send_one(k, _):
            send_across(k, mx, py)
            return 0

        lax.fori_loop(0, chunks, send_one, 0)

    @pl.when(hub)
    def _():
        pl.semaphore_wait(barrier, space_y - 1 + space_x - 1)
        for o in range(1, space_x):
            signal(plane_sem, lax.rem(mx + o, space_x), 0)
        for o in range(half):
            send_line(half + o)
        pl.semaphore_wait(plane_sem, space_x - 1)
        for o in range(1, space_y):
            signal(go_sem, mx, o)

    @pl.when(low)
    def _():
        pl.semaphore_wait(barrier, 1)
        send_line(mirror)
        pl.semaphore_wait(line_sem, half - 1)
        for o in range(1, half):
            send_line(half + lax.rem(mirror - half + o, half))
        pl.semaphore_wait(go_sem, 1)

    @pl.when(high)
    def _():
        pl.semaphore_wait(barrier, half)
        for o in range(1, half):

            @pl.when(o != mirror)
            def _():
                signal(line_sem, mx, o)

        for o in range(half):
            send_line(half - 1 - o)
        pl.semaphore_wait(go_sem, 1)

    def ahead(px, py):
        return jnp.logical_and(px < FIRST, py == 0)

    for c in range(FIRST):

        @pl.when(jnp.logical_and(jnp.logical_or(mx != c, low), me != c * space_y))
        def _():
            send(0, c, 0)

    def send_chunk(k, _):
        def send_next(send_one, px, py):
            piece_k = k + ahead(px, py).astype(jnp.int32)

            @pl.when(piece_k < chunks)
            def _():
                send_one(piece_k, px, py)

        def send_far(i, _):
            oy, ox = split_index(i, space_x - 1)
            send_next(send_across, lax.rem(mx + 1 + ox, space_x), far_y + lax.rem(inner + oy, half))
            return 0

        def send_near(i, _):
            oy, ox = split_index(i, space_x)
            send_next(send, lax.rem(mx + 1 + ox, space_x), near_y + lax.rem(inner + 1 + oy, half))
            return 0

        lax.fori_loop(0, half * (space_x - 1), send_far, 0)
        lax.fori_loop(0, half * space_x - 1, send_near, 0)
        pltpu.make_async_copy(piece(k, mx, my), recv.at[k, me], recv_sem.at[k]).start()
        return 0

    lax.fori_loop(0, chunks, send_chunk, 0)
    fetch_deform.wait()

    lane = lax.broadcasted_iota(jnp.int32, (1, 128), 1)
    spots = [float(q) for q in cheb_nodes(NODES)]

    def node_of(index):
        node = jnp.full((1, 128), spots[0], jnp.float32)
        for t in range(1, NODES):
            node = jnp.where(index == t, spots[t], node)
        return node

    node_x = node_of(lane // NODES % NODES)
    node_y = node_of(lane % NODES)

    def warped(sx, sy, count):
        box = lax.broadcasted_iota(jnp.int32, (count, 128), 0)
        ax = (box // sy).astype(jnp.float32)
        ay = (box % sy).astype(jnp.float32)
        p1 = (ax + node_x) / sx
        p2 = (ay + node_y) / sy
        y1, y2 = 0.0, 0.0
        for m in range(modes):
            y1 = y1 + deform_ref[0, m] * turns((p1 + p2) * (0.5 * (m + 1)))[1]
            y2 = y2 + deform_ref[1, m] * turns((p1 - p2) * (0.5 * (m + 1)))[1]
        return p1 + y1, p2 + y2

    for along, sx, sy, row in steps[1:]:
        count = max(8, sx * sy)
        y1, y2 = warped(sx, sy, count)
        c, s = turns((y1 * (0.25 * sx)) if along == 0 else (y2 * (0.25 * sy)))
        twid[0, pl.ds(row, count), :] = c
        twid[1, pl.ds(row, count), :] = s

    y1, y2 = warped(space_x, space_y, boxes)
    for fx in range(local_x):
        for child in range(2):
            freq = (mx * local_x + fx).astype(jnp.float32) + (0.25 + 0.5 * child)
            c, s = turns(y1 * (freq * gain_x))
            base1[0, 2 * fx + child] = c
            base1[1, 2 * fx + child] = s
    twid[0, pl.ds(0, boxes), :] = y2

    def base_box(i, _):
        freq = lax.broadcasted_iota(jnp.int32, (local_y, 128), 0) + my * local_y
        warp = twid[0, pl.ds(i, 1), :]
        c, s = turns(warp * ((freq.astype(jnp.float32) + 0.5) * gain_y))
        base2[0, i] = c
        base2[1, i] = s
        return 0

    lax.fori_loop(0, boxes, base_box, 0)

    y1, y2 = warped(1, 1, 8)
    out_x = local_x * space_x
    freq = lax.broadcasted_iota(jnp.int32, (out_x, 128), 0) + mx * out_x
    c, s = turns(y1[0:1] * (freq.astype(jnp.float32) + 0.5))
    last1[0] = c
    last1[1] = s
    for child in range(space_y):
        freq = (lax.broadcasted_iota(jnp.int32, (local_y, 128), 0) + my * local_y) * space_y + child
        c, s = turns(y2[0:1] * (freq.astype(jnp.float32) + 0.5))
        last2[0, child] = c
        last2[1, child] = s

    fetch_mix.wait()

    _, _, whole_step, half_steps, finish = butterfly_steps(
        dims, (recv, twid, base1, base2, last1, last2, mix_ref, lhs_high, lhs_low, state)
    )

    def keep(fx, fy, bx, by, re, im):
        spots = pl.ds(fy * (rows * space_y) + by, rows, stride=space_y)
        out_ref[0, fx * space_x + bx, spots, :] = re
        out_ref[1, fx * space_x + bx, spots, :] = im

    def compute(k, _):
        pltpu.make_async_copy(recv.at[k], recv.at[k], recv_sem.at[k]).wait()
        for number in range(len(steps)):
            whole_step(number, k)
        finish(k, keep)
        return 0

    lax.fori_loop(0, chunks - 1, compute, 0)
    some = recv.at[chunks - 1, pl.ds(0, boxes // 2)]
    pltpu.make_async_copy(some, some, recv_sem.at[chunks - 1]).wait()
    near_ref[...] = half_steps(chunks - 1, side)
    pltpu.make_async_copy(some, some, recv_sem.at[chunks]).wait()

    def drain(k, _):
        sent = recv.at[k, pl.ds(0, boxes - 1)]
        pltpu.make_async_copy(sent, sent, send_sem.at[k]).wait()
        return 0

    lax.fori_loop(0, chunks, drain, 0)


def tail_kernel(
    dims,
    done_ref,
    recv,
    twid,
    base1,
    base2,
    last1,
    last2,
    mix_ref,
    near_ref,
    out_hbm,
    lhs_high,
    lhs_low,
    state,
    tail,
    sem,
):
    space_x, space_y, local_x, local_y, rows, _ = dims
    chunks_y = local_y // rows
    last = local_x * chunks_y - 1
    start_x, start_y = (local_x - 1) * space_x, (chunks_y - 1) * rows * space_y
    copies = []

    def copy_out(source, target):
        copies.append(pltpu.make_async_copy(source, target, sem.at[len(copies)]))
        copies[-1].start()

    if start_x:
        spot = (slice(None), pl.ds(0, start_x))
        copy_out(done_ref.at[spot], out_hbm.at[spot])
    if start_y:
        spot = (slice(None), pl.ds(start_x, space_x), pl.ds(0, start_y))
        copy_out(done_ref.at[spot], out_hbm.at[spot])

    total, split, whole_step, half_steps, finish = butterfly_steps(
        dims, (recv, twid, base1, base2, last1, last2, mix_ref, lhs_high, lhs_low, state)
    )
    far = 1 - lax.div(lax.axis_index("sy"), space_y // 2)
    state[...] = near_ref[...] + half_steps(last, far)
    for number in range(split + 1, total):
        whole_step(number, last)

    def keep(fx, fy, bx, by, re, im):
        spots = pl.ds(by, rows, stride=space_y)
        tail[0, bx, spots, :] = re
        tail[1, bx, spots, :] = im

    finish(last, keep)
    spot = (slice(None), pl.ds(start_x, space_x), pl.ds(start_y, rows * space_y))
    copy_out(tail, out_hbm.at[spot])
    for copy in copies:
        copy.wait()


def body(coeffs, deform):
    space_x, space_y = lax.axis_size("sx"), lax.axis_size("sy")
    _, _, freq_x, _, freq_y, lanes = coeffs.shape
    local_x, local_y = freq_x // space_x, freq_y // space_y
    rows = ROWS
    chunks = local_x * local_y // rows
    boxes = space_x * space_y
    out_x, out_y = local_x * space_x, local_y * space_y
    right_sides = lanes // NODES**2
    mix = np.stack([mix_matrix(0, right_sides, NODES), mix_matrix(1, right_sides, NODES)])
    high = mix.astype(jnp.bfloat16)
    low = (mix - high.astype(np.float32)).astype(jnp.bfloat16)
    mix = jnp.asarray(np.concatenate([high, low], axis=2))
    _, twid_rows = plan_of(space_x, space_y)
    dims = (space_x, space_y, local_x, local_y, rows, deform.shape[1])
    vmem = pl.BlockSpec(memory_space=pltpu.VMEM)
    state_rows = boxes * 2 * rows
    f32 = jnp.float32
    tables = [
        pltpu.VMEM((chunks, boxes, 2, rows, lanes), f32),
        pltpu.VMEM((2, twid_rows, lanes), f32),
        pltpu.VMEM((2, 2 * local_x, boxes, lanes), f32),
        pltpu.VMEM((2, boxes, local_y, lanes), f32),
        pltpu.VMEM((2, out_x, lanes), f32),
        pltpu.VMEM((2, space_y, local_y, lanes), f32),
        pltpu.VMEM(mix.shape, mix.dtype),
        pltpu.VMEM((state_rows, lanes), f32),
    ]
    work = [
        pltpu.VMEM((2, state_rows, 2 * lanes), jnp.bfloat16),
        pltpu.VMEM((2, state_rows, 2 * lanes), jnp.bfloat16),
        pltpu.VMEM((state_rows, lanes), f32),
    ]
    results = [pltpu.VMEM((2, out_x, out_y, lanes), f32)] + tables
    held = sum(math.prod(ref.shape) * np.dtype(ref.dtype).itemsize for ref in results)
    partial_out = pl.pallas_call(
        functools.partial(kernel, dims),
        out_shape=results,
        in_specs=[pl.BlockSpec(memory_space=pltpu.HBM)] * 3,
        out_specs=[vmem] * len(results),
        scratch_shapes=work
        + [
            pltpu.SemaphoreType.DMA((chunks,)),
            pltpu.SemaphoreType.DMA((chunks + 1,)),
            pltpu.SMEM(deform.shape, f32),
            pltpu.SemaphoreType.DMA,
            pltpu.SemaphoreType.DMA,
            pltpu.SemaphoreType.REGULAR,
            pltpu.SemaphoreType.REGULAR,
            pltpu.SemaphoreType.REGULAR,
        ],
        compiler_params=pltpu.CompilerParams(
            collective_id=0, has_side_effects=True, vmem_limit_bytes=VMEM_ROOM - held - 65536
        ),
        name="butterfly",
    )(deform, mix, coeffs)
    return pl.pallas_call(
        functools.partial(tail_kernel, dims),
        out_shape=jax.ShapeDtypeStruct((2, out_x, out_y, lanes), f32),
        in_specs=[vmem] * len(results),
        out_specs=pl.BlockSpec(memory_space=pl.ANY),
        scratch_shapes=work
        + [
            pltpu.VMEM((2, space_x, rows * space_y, lanes), f32),
            pltpu.SemaphoreType.DMA((3,)),
        ],
        compiler_params=pltpu.CompilerParams(vmem_limit_bytes=VMEM_ROOM // 4),
        name="tail",
    )(*partial_out)


def solution(mesh):
    placed = (P(None, "sx", None, "sy", None, None), P())
    return jax.shard_map(
        body, mesh=mesh, in_specs=placed, out_specs=P(None, "sx", "sy", None), check_vma=False
    )
```

time: 53.8 us -> 52.2 us (0.970)
  the two profiles are of different devices: /device:TPU:0 before, /device:TPU:9 now
where the time goes in v2:
time: 52.2 us; the launch traced here: 52.1 us
  Pallas kernels  52 us (100%)
    pallas_call x1, Pallas kernels, body(): pl.pallas_call(functools.partial(kernel, dims), out_shape=results, in_spe...  50.1 us
    pallas_call x1, Pallas kernels, body(): pl.pallas_call(functools.partial(tail_kernel, dims), out_shape=jax.ShapeD...  1.91 us

profile of v2, /device:TPU:9, one launch (start us, length us, event | category | flops | bytes accessed | tf_op | source)
XLA Modules:
  0.0 52.1 jit_solution(6446516700474155174)
XLA Ops:
  0.0 50.1 %butterfly.1 = (f32[2,16,128,128]{3,2,1,0:T(8,128)S(1)}, f32[8,32,2,8,128]{4,3,2,1,0:T(8,128)S(1)}, f32[2,72,128]{2,1,0:T(8,128)S(1)}, f32[2,4,32,128]{3,2,1,0:T...) custom-call(f32[2,4]{1,0:T(2,128)} %deform_hbm.1, ...), custom_call_target="tpu_custom_call" | custom-call | tf_op jit(solution)/shard_map/butterfly/pallas_call | solution.py:559
  50.1 1.9 %tail.1 = f32[2,16,128,128]{3,2,1,0:T(8,128)} custom-call(f32[2,16,128,128]{3,2,1,0:T(8,128)S(1)} %get-tuple-element.14.done_ref, f32[8,32,2,8,128]{4,3,2,1,0:T(8,128)S(1)} %get-tuple-element.15.recv, f32[2,72,128]{2,1,0:T(8,128)S(1)} %get-tuple-element.16.twid, f32[2,4,32,128]{3,2,1,0:T(8,128)S(1)} %get-tuple-element.17.base1, ...), custom_call_target="tpu_custom_call" | custom-call | tf_op jit(solution)/shard_map/tail/pallas_call | solution.py:580

commit v3 on v2

--- a/solution.py
+++ b/solution.py
@@ -288,7 +288,7 @@
         pltpu.make_async_remote_copy(
             src_ref=piece(k, px, py),
             dst_ref=recv.at[k, me],
-            send_sem=send_sem.at[k],
+            send_sem=send_sem,
             recv_sem=recv_sem.at[k if lane_sem is None else lane_sem],
             device_id=(px, py),
             device_id_type=MESH,
@@ -337,18 +337,23 @@
             send_line(half - 1 - o)
         pl.semaphore_wait(go_sem, 1)
 
-    def ahead(px, py):
-        return jnp.logical_and(px < FIRST, py == 0)
+    def ahead(px):
+        return jnp.where(px < FIRST, 1, 0)
 
     for c in range(FIRST):
-
-        @pl.when(jnp.logical_and(jnp.logical_or(mx != c, low), me != c * space_y))
-        def _():
-            send(0, c, 0)
+        for o in range(half):
+
+            @pl.when(mx != c)
+            def _():
+                send(0, c, far_y + lax.rem(inner + o, half))
+
+            @pl.when(jnp.logical_or(mx != c, o > 0))
+            def _():
+                send(0, c, near_y + lax.rem(inner + o, half))
 
     def send_chunk(k, _):
         def send_next(send_one, px, py):
-            piece_k = k + ahead(px, py).astype(jnp.int32)
+            piece_k = k + ahead(px)
 
             @pl.when(piece_k < chunks)
             def _():
@@ -452,18 +457,14 @@
         finish(k, keep)
         return 0
 
-    lax.fori_loop(0, chunks - 1, compute, 0)
     some = recv.at[chunks - 1, pl.ds(0, boxes // 2)]
+    lax.fori_loop(0, chunks - 2, compute, 0)
     pltpu.make_async_copy(some, some, recv_sem.at[chunks - 1]).wait()
     near_ref[...] = half_steps(chunks - 1, side)
+    lax.fori_loop(chunks - 2, chunks - 1, compute, 0)
+    sent = recv.at[:, pl.ds(0, boxes - 1)]
+    pltpu.make_async_copy(sent, sent, send_sem).wait()
     pltpu.make_async_copy(some, some, recv_sem.at[chunks]).wait()
-
-    def drain(k, _):
-        sent = recv.at[k, pl.ds(0, boxes - 1)]
-        pltpu.make_async_copy(sent, sent, send_sem.at[k]).wait()
-        return 0
-
-    lax.fori_loop(0, chunks, drain, 0)
 
 
 def tail_kernel(
@@ -563,7 +564,7 @@
         out_specs=[vmem] * len(results),
         scratch_shapes=work
         + [
-            pltpu.SemaphoreType.DMA((chunks,)),
+            pltpu.SemaphoreType.DMA,
             pltpu.SemaphoreType.DMA((chunks + 1,)),
             pltpu.SMEM(deform.shape, f32),
             pltpu.SemaphoreType.DMA,

time: 52.2 us -> 51.5 us (0.987)
  the two profiles are of different devices: /device:TPU:9 before, /device:TPU:0 now
where the time goes in v3:
time: 51.5 us; the launch traced here: 51.1 us
  Pallas kernels  51.1 us (99%)
    pallas_call x1, Pallas kernels, body(): pl.pallas_call(functools.partial(kernel, dims), out_shape=results, in_spe...  49.2 us
    pallas_call x1, Pallas kernels, body(): pl.pallas_call(functools.partial(tail_kernel, dims), out_shape=jax.ShapeD...  1.91 us

profile of v3, /device:TPU:0, one launch (start us, length us, event | category | flops | bytes accessed | tf_op | source)
XLA Modules:
  0.0 51.1 jit_solution(11299703267009376844)
XLA Ops:
  0.0 49.2 %butterfly.1 = (f32[2,16,128,128]{3,2,1,0:T(8,128)S(1)}, f32[8,32,2,8,128]{4,3,2,1,0:T(8,128)S(1)}, f32[2,72,128]{2,1,0:T(8,128)S(1)}, f32[2,4,32,128]{3,2,1,0:T...) custom-call(f32[2,4]{1,0:T(2,128)} %deform_hbm.1, ...), custom_call_target="tpu_custom_call" | custom-call | tf_op jit(solution)/shard_map/butterfly/pallas_call | solution.py:560
  49.2 1.9 %tail.1 = f32[2,16,128,128]{3,2,1,0:T(8,128)} custom-call(f32[2,16,128,128]{3,2,1,0:T(8,128)S(1)} %get-tuple-element.14.done_ref, f32[8,32,2,8,128]{4,3,2,1,0:T(8,128)S(1)} %get-tuple-element.15.recv, f32[2,72,128]{2,1,0:T(8,128)S(1)} %get-tuple-element.16.twid, f32[2,4,32,128]{3,2,1,0:T(8,128)S(1)} %get-tuple-element.17.base1, ...), custom_call_target="tpu_custom_call" | custom-call | tf_op jit(solution)/shard_map/tail/pallas_call | solution.py:581

commit v4 on v3

--- a/solution.py
+++ b/solution.py
@@ -87,7 +87,7 @@
     space_x, space_y, local_x, local_y, rows, _ = dims
     recv, twid, base1, base2, last1, last2, mix_ref, lhs_high, lhs_low, state = refs
     steps, _ = plan_of(space_x, space_y)
-    split = max(n for n, step in enumerate(steps) if step[0] == 1)
+    assert all(step[0] == n % 2 for n, step in enumerate(steps)) and len(steps) % 2 == 1
     chunks_y = local_y // rows
     state_rows = space_x * space_y * 2 * rows
 
@@ -96,13 +96,18 @@
         return fx, fy, pl.ds(pl.multiple_of(fy * rows, 8), rows)
 
     def rotate_into(slot, pair, sibling, size, re0, im0, re1, im1):
-        spot = (slot, pl.ds(pair * 4 * size, 4 * size), pl.ds(128 * sibling, 128))
+        lines = pl.ds(pair * 4 * size, 4 * size)
         whole = jnp.concatenate([re0, im0, re1, im1], axis=0)
         high = whole.astype(jnp.bfloat16)
-        lhs_high[spot] = high
-        lhs_low[spot] = (whole - high.astype(jnp.float32)).astype(jnp.bfloat16)
-
-    def rotate(number, k, first_y, count_y):
+        low = (whole - high.astype(jnp.float32)).astype(jnp.bfloat16)
+        if sibling is None:
+            lhs_high[slot, lines, 0:128] = high
+            lhs_high[slot, lines, 128:256] = low
+        else:
+            lhs_high[slot, lines, pl.ds(128 * sibling, 128)] = high
+            lhs_low[slot, lines, pl.ds(128 * sibling, 128)] = low
+
+    def rotate(number, k, first_y, count_y, alone=False):
         along, sx, sy, row = steps[number]
         fx, _, fy_rows = place(k)
         size = rows << number
@@ -112,7 +117,7 @@
                 if along == 0:
                     pair, sibling = (a1 // 2) * count_y + j, a1 % 2
                 else:
-                    pair, sibling = a1 * (count_y + 1 >> 1) + j // 2, j % 2
+                    pair, sibling = a1 * (count_y + 1 >> 1) + j // 2, None if alone else j % 2
                 if number == 0:
                     re, im = recv[k, table, 0], recv[k, table, 1]
                     c, s = base2[0, table, fy_rows, :], base2[1, table, fy_rows, :]
@@ -148,28 +153,44 @@
         )
         return by_high[:, 0:128] + (by_high[:, 128:256] + by_low)
 
-    def mixed_half(number, side):
+    def mixed_alone(number, sibling, count):
         slot, along = number % 2, steps[number][0]
-        deep = pl.ds(pl.multiple_of(side * 128, 128), 128)
-        by_high = jnp.dot(
-            lhs_high[slot, :, 0:128], mix_ref[along, deep, :], preferred_element_type=jnp.float32
-        )
-        by_low = jnp.dot(
-            lhs_low[slot, :, 0:128], mix_ref[along, deep, 0:128], preferred_element_type=jnp.float32
-        )
-        return by_high[:, 0:128] + (by_high[:, 128:256] + by_low)
+        deep = mix_ref[along, pl.ds(pl.multiple_of(sibling * 128, 128), 128), :]
+        both = jnp.concatenate([deep, deep], axis=0)
+        by = jnp.dot(lhs_high[slot, 0:count], both, preferred_element_type=jnp.float32)
+        return by[:, 0:128] + by[:, 128:256]
 
     def whole_step(number, k):
         rotate(number, k, 0, steps[number][2])
         state[...] = mixed(number, state_rows)
 
-    def half_steps(k, side):
-        for number in range(split):
-            count_y = steps[number][2] // 2
-            rotate(number, k, side * count_y, count_y)
-            state[0 : state_rows // 2] = mixed(number, state_rows // 2)
-        rotate(split, k, side, 1)
-        return mixed_half(split, side)
+    def lone_step(number, k, line):
+        box = lax.div(line, 1 << number // 2)
+        sibling = lax.rem(box, 2)
+        rotate(number, k, box, 1, alone=True)
+        return mixed_alone(number, sibling, steps[number][1] * 4 * (rows << number))
+
+    def subtree(k, line, level):
+        for number in range(2 * level + 1):
+            _, sx, _, _ = steps[number]
+            count_y = (1 << level) >> (number // 2)
+            first_y = lax.div(line, 1 << number // 2)
+            rotate(number, k, first_y, count_y)
+            count = sx * count_y * 2 * (rows << number)
+            state[0:count] = mixed(number, count)
+        return lone_step(2 * level + 1, k, line)
+
+    def late_line(k, line, partials):
+        for number in range(len(steps) - 1):
+            _, sx, _, _ = steps[number]
+            if number % 2:
+                partial = partials[number // 2]
+                state[0 : partial.shape[0]] = partial[...] + lone_step(number, k, line)
+            else:
+                rotate(number, k, lax.div(line, 1 << number // 2), 1)
+                count = sx * 2 * (rows << number)
+                state[0:count] = mixed(number, count)
+        whole_step(len(steps) - 1, k)
 
     def finish(k, store):
         fx, fy, fy_rows = place(k)
@@ -199,7 +220,7 @@
             s = s1 * c2 + c1 * s2
             store(fx, fy, bx, by, re * c - im * s, im * c + re * s)
 
-    return len(steps), split, whole_step, half_steps, finish
+    return len(steps), whole_step, subtree, late_line, finish
 
 
 def kernel(
@@ -215,19 +236,23 @@
     last1,
     last2,
     mix_ref,
-    near_ref,
-    lhs_high,
-    lhs_low,
-    state,
-    send_sem,
-    recv_sem,
-    deform_ref,
-    deform_sem,
-    mix_sem,
-    plane_sem,
-    go_sem,
-    line_sem,
+    *refs,
 ):
+    levels = (dims[1] - 1).bit_length()
+    partials = refs[:levels]
+    (
+        lhs_high,
+        lhs_low,
+        state,
+        send_sem,
+        recv_sem,
+        deform_ref,
+        deform_sem,
+        mix_sem,
+        plane_sem,
+        go_sem,
+        line_sem,
+    ) = refs[levels:]
     space_x, space_y, local_x, local_y, rows, modes = dims
     steps, _ = plan_of(space_x, space_y)
     chunks_y = local_y // rows
@@ -246,6 +271,7 @@
     far_y = (1 - side) * half
     mirror = space_y - 1 - my
     hub = my == 0
+    at_edge = inner == (half - 1) * (1 - side)
     low = jnp.logical_and(side == 0, my > 0)
     high = side == 1
 
@@ -295,7 +321,7 @@
         ).start()
 
     def send_across(k, px, py):
-        send(k, px, py, jnp.where(k == chunks - 1, chunks, k))
+        send(k, px, py, jnp.where(k == chunks - 1, jnp.where(at_edge, chunks + 1, chunks), k))
 
     def send_line(py):
         def send_one(k, _):
@@ -361,7 +387,7 @@
 
         def send_far(i, _):
             oy, ox = split_index(i, space_x - 1)
-            send_next(send_across, lax.rem(mx + 1 + ox, space_x), far_y + lax.rem(inner + oy, half))
+            send_next(send_across, jnp.bitwise_xor(mx, space_x - 1 - ox), far_y + lax.rem(inner + oy, half))
             return 0
 
         def send_near(i, _):
@@ -441,7 +467,7 @@
 
     fetch_mix.wait()
 
-    _, _, whole_step, half_steps, finish = butterfly_steps(
+    total, whole_step, subtree, _, finish = butterfly_steps(
         dims, (recv, twid, base1, base2, last1, last2, mix_ref, lhs_high, lhs_low, state)
     )
 
@@ -452,19 +478,29 @@
 
     def compute(k, _):
         pltpu.make_async_copy(recv.at[k], recv.at[k], recv_sem.at[k]).wait()
-        for number in range(len(steps)):
+        for number in range(total):
             whole_step(number, k)
         finish(k, keep)
         return 0
 
-    some = recv.at[chunks - 1, pl.ds(0, boxes // 2)]
-    lax.fori_loop(0, chunks - 2, compute, 0)
-    pltpu.make_async_copy(some, some, recv_sem.at[chunks - 1]).wait()
-    near_ref[...] = half_steps(chunks - 1, side)
-    lax.fori_loop(chunks - 2, chunks - 1, compute, 0)
+    last = chunks - 1
+    near = recv.at[last, pl.ds(0, boxes // 2)]
+    outer = recv.at[last, pl.ds(0, (half - 1) * space_x)]
+    edge = recv.at[last, pl.ds(0, space_x)]
+    first, second = max(last - 2, 0), max(last - 1, 0)
+    lax.fori_loop(0, first, compute, 0)
+    pltpu.make_async_copy(near, near, recv_sem.at[last]).wait()
+    partials[-1][...] = subtree(last, near_y, levels - 1)
+    lax.fori_loop(first, second, compute, 0)
+    if half > 1:
+        pltpu.make_async_copy(outer, outer, recv_sem.at[chunks]).wait()
+    for level in range(levels - 1):
+        line = half + (1 << level) - side * (3 << level)
+        partials[level][...] = subtree(last, line, level)
+    lax.fori_loop(second, last, compute, 0)
     sent = recv.at[:, pl.ds(0, boxes - 1)]
     pltpu.make_async_copy(sent, sent, send_sem).wait()
-    pltpu.make_async_copy(some, some, recv_sem.at[chunks]).wait()
+    pltpu.make_async_copy(edge, edge, recv_sem.at[chunks + 1]).wait()
 
 
 def tail_kernel(
@@ -477,14 +513,11 @@
     last1,
     last2,
     mix_ref,
-    near_ref,
-    out_hbm,
-    lhs_high,
-    lhs_low,
-    state,
-    tail,
-    sem,
+    *refs,
 ):
+    levels = (dims[1] - 1).bit_length()
+    partials = refs[:levels]
+    out_hbm, lhs_high, lhs_low, state, tail, sem = refs[levels:]
     space_x, space_y, local_x, local_y, rows, _ = dims
     chunks_y = local_y // rows
     last = local_x * chunks_y - 1
@@ -502,13 +535,12 @@
         spot = (slice(None), pl.ds(start_x, space_x), pl.ds(0, start_y))
         copy_out(done_ref.at[spot], out_hbm.at[spot])
 
-    total, split, whole_step, half_steps, finish = butterfly_steps(
+    _, _, _, late_line, finish = butterfly_steps(
         dims, (recv, twid, base1, base2, last1, last2, mix_ref, lhs_high, lhs_low, state)
     )
-    far = 1 - lax.div(lax.axis_index("sy"), space_y // 2)
-    state[...] = near_ref[...] + half_steps(last, far)
-    for number in range(split + 1, total):
-        whole_step(number, last)
+    half = space_y // 2
+    side = lax.div(lax.axis_index("sy"), half)
+    late_line(last, half - side, partials)
 
     def keep(fx, fy, bx, by, re, im):
         spots = pl.ds(by, rows, stride=space_y)
@@ -548,7 +580,11 @@
         pltpu.VMEM((2, out_x, lanes), f32),
         pltpu.VMEM((2, space_y, local_y, lanes), f32),
         pltpu.VMEM(mix.shape, mix.dtype),
-        pltpu.VMEM((state_rows, lanes), f32),
+    ]
+    tables += [
+        pltpu.VMEM((sx * 4 * (rows << number), lanes), f32)
+        for number, (along, sx, _, _) in enumerate(plan_of(space_x, space_y)[0])
+        if along == 1
     ]
     work = [
         pltpu.VMEM((2, state_rows, 2 * lanes), jnp.bfloat16),
@@ -565,7 +601,7 @@
         scratch_shapes=work
         + [
             pltpu.SemaphoreType.DMA,
-            pltpu.SemaphoreType.DMA((chunks + 1,)),
+            pltpu.SemaphoreType.DMA((chunks + 2,)),
             pltpu.SMEM(deform.shape, f32),
             pltpu.SemaphoreType.DMA,
             pltpu.SemaphoreType.DMA,

time: 51.5 us -> 51.2 us (level)
  no operation moved by 1% of the time
where the time goes in v4:
time: 51.2 us; the launch traced here: 51 us
  Pallas kernels  51 us (100%)
    pallas_call x1, Pallas kernels, body(): pl.pallas_call(functools.partial(kernel, dims), out_shape=results, in_spe...  49.2 us
    pallas_call x1, Pallas kernels, body(): pl.pallas_call(functools.partial(tail_kernel, dims), out_shape=jax.ShapeD...  1.8 us

profile of v4, /device:TPU:0, one launch (start us, length us, event | category | flops | bytes accessed | tf_op | source)
XLA Modules:
  0.0 51.0 jit_solution(2549153098354255346)
XLA Ops:
  0.0 49.2 %butterfly.1 = (f32[2,16,128,128]{3,2,1,0:T(8,128)S(1)}, f32[8,32,2,8,128]{4,3,2,1,0:T(8,128)S(1)}, f32[2,72,128]{2,1,0:T(8,128)S(1)}, f32[2,4,32,128]{3,2,1,0:T...) custom-call(f32[2,4]{1,0:T(2,128)} %deform_hbm.1, ...), custom_call_target="tpu_custom_call" | custom-call | tf_op jit(solution)/shard_map/butterfly/pallas_call | solution.py:596
  49.2 1.8 %tail.1 = f32[2,16,128,128]{3,2,1,0:T(8,128)} custom-call(f32[2,16,128,128]{3,2,1,0:T(8,128)S(1)} %get-tuple-element.15.done_ref, f32[8,32,2,8,128]{4,3,2,1,0:T(8,128)S(1)} %get-tuple-element.16.recv, f32[2,72,128]{2,1,0:T(8,128)S(1)} %get-tuple-element.17.twid, f32[2,4,32,128]{3,2,1,0:T(8,128)S(1)} %get-tuple-element.18.base1, ...), custom_call_target="tpu_custom_call" | custom-call | tf_op jit(solution)/shard_map/tail/pallas_call | solution.py:617

commit v5 on v4

--- a/solution.py
+++ b/solution.py
@@ -85,7 +85,7 @@
 
 def butterfly_steps(dims, refs):
     space_x, space_y, local_x, local_y, rows, _ = dims
-    recv, twid, base1, base2, last1, last2, mix_ref, lhs_high, lhs_low, state = refs
+    recv, twid, base1, base2, last1, last2, mix_ref, lhs, state = refs
     steps, _ = plan_of(space_x, space_y)
     assert all(step[0] == n % 2 for n, step in enumerate(steps)) and len(steps) % 2 == 1
     chunks_y = local_y // rows
@@ -97,15 +97,12 @@
 
     def rotate_into(slot, pair, sibling, size, re0, im0, re1, im1):
         lines = pl.ds(pair * 4 * size, 4 * size)
-        whole = jnp.concatenate([re0, im0, re1, im1], axis=0)
+        lane = 128 * (sibling or 0)
+        lhs[slot, lines, lane : lane + 128] = jnp.concatenate([re0, im0, re1, im1], axis=0)
+
+    def parted(whole):
         high = whole.astype(jnp.bfloat16)
-        low = (whole - high.astype(jnp.float32)).astype(jnp.bfloat16)
-        if sibling is None:
-            lhs_high[slot, lines, 0:128] = high
-            lhs_high[slot, lines, 128:256] = low
-        else:
-            lhs_high[slot, lines, pl.ds(128 * sibling, 128)] = high
-            lhs_low[slot, lines, pl.ds(128 * sibling, 128)] = low
+        return high, (whole - high.astype(jnp.float32)).astype(jnp.bfloat16)
 
     def rotate(number, k, first_y, count_y, alone=False):
         along, sx, sy, row = steps[number]
@@ -145,19 +142,17 @@
 
     def mixed(number, count):
         slot, along = number % 2, steps[number][0]
-        by_high = jnp.dot(
-            lhs_high[slot, 0:count], mix_ref[along], preferred_element_type=jnp.float32
-        )
-        by_low = jnp.dot(
-            lhs_low[slot, 0:count], mix_ref[along, :, 0:128], preferred_element_type=jnp.float32
-        )
+        high, low = parted(lhs[slot, 0:count])
+        by_high = jnp.dot(high, mix_ref[along], preferred_element_type=jnp.float32)
+        by_low = jnp.dot(low, mix_ref[along, :, 0:128], preferred_element_type=jnp.float32)
         return by_high[:, 0:128] + (by_high[:, 128:256] + by_low)
 
     def mixed_alone(number, sibling, count):
         slot, along = number % 2, steps[number][0]
         deep = mix_ref[along, pl.ds(pl.multiple_of(sibling * 128, 128), 128), :]
         both = jnp.concatenate([deep, deep], axis=0)
-        by = jnp.dot(lhs_high[slot, 0:count], both, preferred_element_type=jnp.float32)
+        pair = jnp.concatenate(parted(lhs[slot, 0:count, 0:128]), axis=1)
+        by = jnp.dot(pair, both, preferred_element_type=jnp.float32)
         return by[:, 0:128] + by[:, 128:256]
 
     def whole_step(number, k):
@@ -241,8 +236,7 @@
     levels = (dims[1] - 1).bit_length()
     partials = refs[:levels]
     (
-        lhs_high,
-        lhs_low,
+        lhs,
         state,
         send_sem,
         recv_sem,
@@ -468,7 +462,7 @@
     fetch_mix.wait()
 
     total, whole_step, subtree, _, finish = butterfly_steps(
-        dims, (recv, twid, base1, base2, last1, last2, mix_ref, lhs_high, lhs_low, state)
+        dims, (recv, twid, base1, base2, last1, last2, mix_ref, lhs, state)
     )
 
     def keep(fx, fy, bx, by, re, im):
@@ -517,7 +511,7 @@
 ):
     levels = (dims[1] - 1).bit_length()
     partials = refs[:levels]
-    out_hbm, lhs_high, lhs_low, state, tail, sem = refs[levels:]
+    out_hbm, lhs, state, tail, sem = refs[levels:]
     space_x, space_y, local_x, local_y, rows, _ = dims
     chunks_y = local_y // rows
     last = local_x * chunks_y - 1
@@ -536,7 +530,7 @@
         copy_out(done_ref.at[spot], out_hbm.at[spot])
 
     _, _, _, late_line, finish = butterfly_steps(
-        dims, (recv, twid, base1, base2, last1, last2, mix_ref, lhs_high, lhs_low, state)
+        dims, (recv, twid, base1, base2, last1, last2, mix_ref, lhs, state)
     )
     half = space_y // 2
     side = lax.div(lax.axis_index("sy"), half)
@@ -587,8 +581,7 @@
         if along == 1
     ]
     work = [
-        pltpu.VMEM((2, state_rows, 2 * lanes), jnp.bfloat16),
-        pltpu.VMEM((2, state_rows, 2 * lanes), jnp.bfloat16),
+        pltpu.VMEM((2, state_rows, 2 * lanes), f32),
         pltpu.VMEM((state_rows, lanes), f32),
     ]
     results = [pltpu.VMEM((2, out_x, out_y, lanes), f32)] + tables

time: 51.2 us -> 51.1 us (level)
  no operation moved by 1% of the time
where the time goes in v5:
time: 51.1 us; the launch traced here: 50.9 us
  Pallas kernels  50.9 us (100%)
    pallas_call x1, Pallas kernels, body(): pl.pallas_call(functools.partial(kernel, dims), out_shape=results, in_spe...  49.2 us
    pallas_call x1, Pallas kernels, body(): pl.pallas_call(functools.partial(tail_kernel, dims), out_shape=jax.ShapeD...  1.7 us

profile of v5, /device:TPU:0, one launch (start us, length us, event | category | flops | bytes accessed | tf_op | source)
XLA Modules:
  0.0 50.9 jit_solution(15831071296938125644)
XLA Ops:
  0.0 49.2 %butterfly.1 = (f32[2,16,128,128]{3,2,1,0:T(8,128)S(1)}, f32[8,32,2,8,128]{4,3,2,1,0:T(8,128)S(1)}, f32[2,72,128]{2,1,0:T(8,128)S(1)}, f32[2,4,32,128]{3,2,1,0:T...) custom-call(f32[2,4]{1,0:T(2,128)} %deform_hbm.1, ...), custom_call_target="tpu_custom_call" | custom-call | tf_op jit(solution)/shard_map/butterfly/pallas_call | solution.py:589
  49.2 1.7 %tail.1 = f32[2,16,128,128]{3,2,1,0:T(8,128)} custom-call(f32[2,16,128,128]{3,2,1,0:T(8,128)S(1)} %get-tuple-element.15.done_ref, f32[8,32,2,8,128]{4,3,2,1,0:T(8,128)S(1)} %get-tuple-element.16.recv, f32[2,72,128]{2,1,0:T(8,128)S(1)} %get-tuple-element.17.twid, f32[2,4,32,128]{3,2,1,0:T(8,128)S(1)} %get-tuple-element.18.base1, ...), custom_call_target="tpu_custom_call" | custom-call | tf_op jit(solution)/shard_map/tail/pallas_call | solution.py:610

commit v6 on v5

--- a/solution.py
+++ b/solution.py
@@ -357,8 +357,8 @@
             send_line(half - 1 - o)
         pl.semaphore_wait(go_sem, 1)
 
-    def ahead(px):
-        return jnp.where(px < FIRST, 1, 0)
+    def ahead(px, py):
+        return jnp.where(px < FIRST, jnp.where(py == 0, 2, 1), 0)
 
     for c in range(FIRST):
         for o in range(half):
@@ -371,9 +371,19 @@
             def _():
                 send(0, c, near_y + lax.rem(inner + o, half))
 
+    for c in range(FIRST):
+
+        @pl.when(jnp.logical_and(high, mx != c))
+        def _():
+            send_across(1, c, 0)
+
+        @pl.when(jnp.logical_and(side == 0, jnp.logical_or(mx != c, low)))
+        def _():
+            send(1, c, 0)
+
     def send_chunk(k, _):
         def send_next(send_one, px, py):
-            piece_k = k + ahead(px)
+            piece_k = k + ahead(px, py)
 
             @pl.when(piece_k < chunks)
             def _():

time: 51.1 us -> 51 us (level)
  the two profiles are of different devices: /device:TPU:0 before, /device:TPU:4 now
where the time goes in v6:
time: 51 us; the launch traced here: 50.8 us
  Pallas kernels  50.8 us (100%)
    pallas_call x1, Pallas kernels, body(): pl.pallas_call(functools.partial(kernel, dims), out_shape=results, in_spe...  49.1 us
    pallas_call x1, Pallas kernels, body(): pl.pallas_call(functools.partial(tail_kernel, dims), out_shape=jax.ShapeD...  1.7 us

profile of v6, /device:TPU:4, one launch (start us, length us, event | category | flops | bytes accessed | tf_op | source)
XLA Modules:
  0.0 50.8 jit_solution(18040335896271551486)
XLA Ops:
  0.0 49.1 %butterfly.1 = (f32[2,16,128,128]{3,2,1,0:T(8,128)S(1)}, f32[8,32,2,8,128]{4,3,2,1,0:T(8,128)S(1)}, f32[2,72,128]{2,1,0:T(8,128)S(1)}, f32[2,4,32,128]{3,2,1,0:T...) custom-call(f32[2,4]{1,0:T(2,128)} %deform_hbm.1, ...), custom_call_target="tpu_custom_call" | custom-call | tf_op jit(solution)/shard_map/butterfly/pallas_call | solution.py:599
  49.1 1.7 %tail.1 = f32[2,16,128,128]{3,2,1,0:T(8,128)} custom-call(f32[2,16,128,128]{3,2,1,0:T(8,128)S(1)} %get-tuple-element.15.done_ref, f32[8,32,2,8,128]{4,3,2,1,0:T(8,128)S(1)} %get-tuple-element.16.recv, f32[2,72,128]{2,1,0:T(8,128)S(1)} %get-tuple-element.17.twid, f32[2,4,32,128]{3,2,1,0:T(8,128)S(1)} %get-tuple-element.18.base1, ...), custom_call_target="tpu_custom_call" | custom-call | tf_op jit(solution)/shard_map/tail/pallas_call | solution.py:620
